TPU v7x, 32 devices: a whole 2x2x4 slice. The times are simulated.
32 devices in a mesh: grp: 2 (over y), ka: 4 (over z), ga: 2 (over x), ba: 2 (over core).
Axes of the slice: x: 2, y: 2, z: 4, core: 2. Of those that a mesh axis runs over, the one named last changes fastest.
Arguments:
- coefficients: bfloat16 [2, 2, 16, 512, 9216], P(None, None, ('grp', 'ka'), 'ba', 'ga'), parts along dimension 2, may hold values from -1 to 1
- occupied: int32 [2, 16], P(None, ('grp', 'ka')), parts along dimension 1, may hold values from 64 to 512
- kweights: float32 [16], P(('grp', 'ka')), parts along dimension 0, may hold values from 0.5 to 2
- owner_map: int32 [1024], P('grp'), parts along dimension 0, may hold values from 0 to 7, as said below
- species: int32 [1024], P('grp'), parts along dimension 0, may hold values from 0 to 1
- positions: float32 [3, 1024], P(None, 'grp'), parts along dimension 1, may hold values from 0 to 100
- multipole: float32 [2, 9, 324], replicated, may hold values from -0.3125 to 0.3125
- widths: float32 [2], replicated, may hold values from 0.05 to 0.3
- potential: float32 [2, 442368], P(None, ('grp', 'ga')), parts along dimension 1, may hold values from -0.013671875 to 0.013671875
Outputs:
- density: float32 [2, 2, 1024, 324], P(None, None, ('grp', 'ka', 'ga', 'ba')), parts along dimension 2
- forces: float32 [3, 1024], P(None, ('grp', 'ka', 'ga', 'ba')), parts along dimension 1
There are 2 independent parts, one for each index of `grp`. A program takes and returns all parts, laid end to end along the dimension named above; an argument that names none is the same for every part. Nothing has to cross between parts.
Inputs may be any that keep to these rules, and one draw needn't show every extreme that they name: `owner_map`: within each aligned block of 256 atoms every owner number is named by exactly 32 atoms.
All inputs are finite; a program needn't handle non-finite values.
Results may differ from a plain program's by a relative error of at most 0.0003.
Values sent between devices are 32-bit elements; how exact they have to be, the bound alone decides.
A program may use at most 192 MiB of HBM per device.

v0:
```python
import jax
import jax.numpy as jnp
from jax import lax
from jax.sharding import PartitionSpec as P

NPROJ = 18
SPECIES = 2
NL = 9
GRID = 96
grid_step = 0.0625
highest = lax.Precision.HIGHEST


def harmonics(start_index, length, widths):
    indices = start_index + jnp.arange(length, dtype=jnp.int32)
    planes = [indices % GRID, indices // GRID % GRID, indices // (GRID * GRID)]
    vectors = []
    for plane_index in planes:
        signed = jnp.where(plane_index >= GRID // 2, plane_index - GRID, plane_index)
        vectors.append(grid_step * signed.astype(jnp.float32))
    along_x, along_y, along_z = vectors
    square = along_x * along_x + along_y * along_y + along_z * along_z
    shapes = jnp.stack(
        [
            jnp.ones_like(square),
            along_x,
            along_y,
            along_z,
            along_x * along_y,
            along_y * along_z,
            along_z * along_x,
            along_x * along_x - along_y * along_y,
            3.0 * along_z * along_z - square,
        ]
    )
    damping = jnp.exp(-widths[:, None] * square[None, :])
    form_table = (damping[:, None, :] * shapes[None, :, :]).reshape(SPECIES * NL, length)
    return (form_table, jnp.stack(vectors, axis=1))


def force_block(moments, places, form_table, vectors, pot_piece):
    smooth = jnp.dot(moments, form_table, precision=highest)
    phases = jnp.dot(places, vectors.T, precision=highest)
    wave_term = pot_piece[0][None, :] * jnp.sin(phases) + pot_piece[1][None, :] * jnp.cos(phases)
    return jnp.dot(smooth * wave_term, vectors, precision=highest)


def local_force(moments, places, pot_piece, start_index, widths):
    length = pot_piece.shape[1]
    pieces = 8
    width_block = length // pieces

    def gblock(running, number):
        offset = number * width_block
        form_table, vectors = harmonics(start_index + offset, width_block, widths)
        segment = lax.dynamic_slice_in_dim(pot_piece, offset, width_block, 1)
        return (running + force_block(moments, places, form_table, vectors, segment), None)

    result, unused = lax.scan(
        gblock, jnp.zeros((moments.shape[0], 3), jnp.float32), jnp.arange(pieces, dtype=jnp.int32)
    )
    return result


def shards(
    coefficients, occupied, kweights, owner_map, species, positions, multipole, widths, potential
):
    spin_count, complex_parts, kcount, bcount, columns = coefficients.shape
    atoms_blk = columns // NPROJ
    kgroups = lax.axis_size("ka")
    bgroups = lax.axis_size("ba")
    owners = kgroups * bgroups
    per_owner = atoms_blk // owners
    owner_index = lax.axis_index(("ka", "ba"))
    group_index = lax.axis_index("ga")
    band_index = lax.axis_index("ba") * bcount + jnp.arange(bcount, dtype=jnp.int32)
    band_mask = (band_index[None, None, :] < occupied[:, :, None]).astype(jnp.bfloat16)
    values = coefficients.reshape(spin_count, complex_parts, kcount, bcount, atoms_blk, NPROJ)
    masked = values * band_mask[:, None, :, :, None, None]
    real_part = jnp.einsum(
        "sckbai,sckbaj->skaij", values, masked, preferred_element_type=jnp.float32
    )
    cross_term = jnp.einsum(
        "skbai,skbaj->skaij", values[:, 0], masked[:, 1], preferred_element_type=jnp.float32
    )
    imag_part = cross_term - jnp.swapaxes(cross_term, 3, 4)
    weighted = jnp.stack([real_part, imag_part], axis=1) * kweights[None, None, :, None, None, None]
    density_local = jnp.sum(weighted, axis=2).reshape(
        spin_count, complex_parts, atoms_blk, NPROJ * NPROJ
    )
    ranking = jnp.argsort(owner_map.reshape(-1, atoms_blk), axis=1, stable=True)
    own_ranks = lax.dynamic_slice_in_dim(ranking, owner_index * per_owner, per_owner, 1)
    summed = lax.psum(density_local, ("ka", "ba"))
    own_rows = lax.dynamic_index_in_dim(own_ranks, group_index, 0, keepdims=False)
    own_density = jnp.take(summed, own_rows, axis=2)
    block_count = own_ranks.shape[0]
    atom_ids = jnp.arange(block_count, dtype=jnp.int32)[:, None] * atoms_blk + own_ranks
    own_atoms = lax.dynamic_index_in_dim(atom_ids, group_index, 0, keepdims=False)
    real_total = jnp.sum(own_density[:, 0], axis=0)
    selector = (
        jnp.take(species, own_atoms)[:, None] == jnp.arange(SPECIES, dtype=jnp.int32)[None, :]
    ).astype(jnp.float32)
    moments = jnp.dot(
        real_total, multipole.reshape(SPECIES * NL, NPROJ * NPROJ).T, precision=highest
    ) * jnp.repeat(selector, NL, axis=1)
    gcount = potential.shape[1]
    all_moments = lax.all_gather(moments, "ga", axis=0, tiled=True)
    places = jnp.take(positions, atom_ids.reshape(-1), axis=1).T
    partial_force = local_force(all_moments, places, potential, group_index * gcount, widths)
    summed_force = lax.psum(partial_force, "ga")
    own_force = lax.dynamic_slice_in_dim(summed_force, group_index * per_owner, per_owner, 0)
    return (own_density, own_force.T)


def solution(mesh):
    placed = (
        P(None, None, ("grp", "ka"), "ba", "ga"),
        P(None, ("grp", "ka")),
        P(("grp", "ka")),
        P("grp"),
        P("grp"),
        P(None, "grp"),
        P(),
        P(),
        P(None, ("grp", "ga")),
    )
    return jax.shard_map(
        shards,
        mesh=mesh,
        in_specs=placed,
        out_specs=(
            P(None, None, ("grp", "ka", "ga", "ba"), None),
            P(None, ("grp", "ka", "ga", "ba")),
        ),
        check_vma=False,
    )
```

profile of v0, /device:TPU:0, one launch (start us, length us, event | category | flops | bytes accessed | tf_op | source)
XLA Modules:
  0.0 663.2 jit_solution(12733213700706561287)
XLA Ops:
  10.0 45.7 %copy.45 = bf16[2,2,2,256,4608]{3,2,4,1,0:T(2,128)(2,1)} copy(bf16[2,2,2,256,4608]{4,3,2,1,0:T(8,128)(2,1)} %param.11) | data formatting | bytes 37748736 | tf_op args[0]
  55.7 45.4 %copy.46 = bf16[2,2,2,256,256,18]{4,3,5,2,1,0:T(8,128)(2,1)} copy(bf16[2,2,2,256,256,18]{3,2,5,4,1,0:T(2,128)(2,1)} %bitcast.68) | data formatting | bytes 37748736 | tf_op jit(solution)/shard_map/reshape | solution.py:78
  101.1 9.1 %slice.35 = bf16[2,1,2,256,256,18]{3,2,5,4,1,0:T(2,128)(2,1)} slice(bf16[2,2,2,256,256,18]{3,2,5,4,1,0:T(2,128)(2,1)} %bitcast.69), slice={[0:2], [0:1], [0:2], [0:256], [0:256], [0:18]} | slice | bytes 18874368 | tf_op jit(solution)/shard_map/slice | solution.py:84
  110.3 16.7 %broadcast_multiply_fusion.2 = bf16[2,2,2,256,256,18]{4,3,5,2,1,0:T(8,128)(2,1)} fusion(bf16[2,2,2,256,256,18]{4,3,5,2,1,0:T(8,128)(2,1)} %copy.46, bf16[2,2,256]{2,1,0:T(2,128)(2,1)S(1)} %compare_convert_fusion), kind=kLoop, calls=%fused_computation.84 | loop fusion | flops 9437184 | bytes 37750784 | tf_op jit(solution)/shard_map/mul | solution.py:79
  127.0 8.4 %slice_bitcast_fusion = bf16[2,2,256,256,18]{3,2,4,1,0:T(8,128)(2,1)} fusion(bf16[2,2,2,256,256,18]{4,3,5,2,1,0:T(8,128)(2,1)} %broadcast_multiply_fusion.2), kind=kLoop, calls=%fused_computation.83 | loop fusion | bytes 18874368 | tf_op jit(solution)/shard_map/squeeze | solution.py:84
  135.4 29.6 %copy.62 = bf16[2,2,2,256,256,18]{3,5,1,2,0,4:T(8,128)(2,1)} copy(bf16[2,2,2,256,256,18]{4,3,5,2,1,0:T(8,128)(2,1)} %broadcast_multiply_fusion.2) | data formatting | bytes 37748736 | tf_op jit(solution)/shard_map/mul | solution.py:79
  165.1 15.5 %copy.50 = bf16[2,2,256,256,18]{2,4,3,1,0:T(8,128)(2,1)} copy(bf16[2,2,256,256,18]{3,2,4,1,0:T(8,128)(2,1)} %slice_bitcast_fusion) | data formatting | bytes 18874368 | tf_op jit(solution)/shard_map/squeeze | solution.py:84
  180.6 13.3 %fusion.40 = f32[2,2,256,18,18]{4,3,2,1,0:T(8,128)} fusion(bf16[2,2,256,256,18]{2,4,3,1,0:T(8,128)(2,1)} %copy.50, bf16[2,1,2,256,256,18]{3,2,5,4,1,0:T(2,128)(2,1)} %slice.35), kind=kOutput, calls=%fused_computation.80 | convolution fusion | flops 169869312 | bytes 20201472 | tf_op jit(solution)/shard_map/skbai,skbaj->skaij/dot_general | solution.py:83
  193.9 14.0 %copy.51 = f32[2,2,256,18,18]{3,4,2,1,0:T(8,128)} copy(f32[2,2,256,18,18]{4,3,2,1,0:T(8,128)} %fusion.40) | data formatting | bytes 2654208 | tf_op jit(solution)/shard_map/skbai,skbaj->skaij/dot_general | solution.py:83
  207.9 14.1 %fusion.41 = f32[2,1,2,256,18,18]{5,4,3,2,0,1:T(8,128)} fusion(f32[2,2,256,18,18]{4,3,2,1,0:T(8,128)} %fusion.40, f32[2,2,256,18,18]{3,4,2,1,0:T(8,128)} %copy.51), kind=kLoop, calls=%fused_computation.82 | loop fusion | flops 331776 | bytes 3981312 | tf_op jit(solution)/shard_map/stack | solution.py:87
  221.9 11.4 %copy.53 = f32[2,1,2,256,18,18]{3,2,5,4,1,0:T(2,128)S(1)} copy(f32[2,1,2,256,18,18]{5,4,3,2,0,1:T(8,128)} %fusion.41) | data formatting | bytes 2654208 | tf_op jit(solution)/shard_map/stack | solution.py:87
  233.4 21.8 %fusion.42 = f32[2,1,2,256,18,18]{4,5,2,0,3,1:T(8,128)} fusion(bf16[2,2,2,256,256,18]{3,5,1,2,0,4:T(8,128)(2,1)} %copy.62, bf16[2,2,2,256,256,18]{3,2,5,4,1,0:T(2,128)(2,1)} %bitcast.70), kind=kOutput, calls=%fused_computation.85 | convolution fusion | flops 339738624 | bytes 39075840 | tf_op jit(solution)/shard_map/sckbai,sckbaj->skaij/dot_general | solution.py:80
  255.1 11.6 %copy.52 = f32[2,1,2,256,18,18]{3,2,5,4,1,0:T(2,128)S(1)} copy(f32[2,1,2,256,18,18]{4,5,2,0,3,1:T(8,128)} %fusion.42) | data formatting | bytes 2654208 | tf_op jit(solution)/shard_map/stack | solution.py:87
  266.8 3.7 fusion.45
  271.6 2.4 copy.56
  278.9 60.1 %all-reduce.2.cloned.1.call-done = f32[2,2,256,324]{3,1,2,0:T(2,128)} async-done(((f32[2,2,256,324]{3,1,2,0:T(2,128)}), f32[2,2,256,324]{3,1,2,0:T(2,128)}) %all-reduce.2.cloned.1.call-update) | async-done | bytes 1327120 | tf_op jit(solution)/shard_map/psum | solution.py:93
  339.0 2.2 gather_fusion
  342.3 4.4 all-gather
  346.8 303.3 %while.14 = (s32[]{:T(128)}, f32[64,3]{0,1:T(4,128)}, f32[2,1]{0,1:T(1,128)S(1)}, s32[8]{0:T(128)S(1)}, s32[]{:T(128)}, /*index=5*/f32[64,18]{0,1:T(8,128)S(1)},...) while((s32[]{:T(128)}, f32[64,3]{0,1:T(4,128)}, ...), condition=%wide.region_5.6_spmd.clone, body=%wide.region_4.5_spmd.clone.sunk | while | flops 262103424 | bytes 21960220 | solution.py:59
  356.1 3.7 fusion.77
  359.8 1.3 dynamic-slice_reduce_fusion.3
  361.2 18.2 %convolution_multiply_fusion.3 = f32[13824,64]{0,1:T(8,128)} fusion(f32[18,13824]{1,0:T(8,128)} %mul.712, f32[64,18]{0,1:T(8,128)S(1)} %get-tuple-element.353, f32[13824,64]{0,1:T(8,128)S(1)} %fusion.77, f32[13824]{0:T(1024)S(1)} %get-tuple-element.318, f32[13824]{0:T(1024)S(1)} %get-tuple-element.319), kind=kOutput, calls=%fused_computation.3.clone.1 | convolution fusion | flops 194641920 | bytes 8188416 | tf_op jit(solution)/shard_map/while/body/eval_jaxpr/dot_general | solution.py:42
  379.4 5.5 convolution_add_fusion.2
  394.0 3.7 fusion.77
  397.7 1.3 dynamic-slice_reduce_fusion.3
  399.1 18.2 %convolution_multiply_fusion.3 = f32[13824,64]{0,1:T(8,128)} fusion(f32[18,13824]{1,0:T(8,128)} %mul.712, f32[64,18]{0,1:T(8,128)S(1)} %get-tuple-element.353, f32[13824,64]{0,1:T(8,128)S(1)} %fusion.77, f32[13824]{0:T(1024)S(1)} %get-tuple-element.318, f32[13824]{0:T(1024)S(1)} %get-tuple-element.319), kind=kOutput, calls=%fused_computation.3.clone.1 | convolution fusion | flops 194641920 | bytes 8188416 | tf_op jit(solution)/shard_map/while/body/eval_jaxpr/dot_general | solution.py:42
  417.3 5.5 convolution_add_fusion.2
  431.9 3.7 fusion.77
  435.6 1.3 dynamic-slice_reduce_fusion.3
  436.9 18.2 %convolution_multiply_fusion.3 = f32[13824,64]{0,1:T(8,128)} fusion(f32[18,13824]{1,0:T(8,128)} %mul.712, f32[64,18]{0,1:T(8,128)S(1)} %get-tuple-element.353, f32[13824,64]{0,1:T(8,128)S(1)} %fusion.77, f32[13824]{0:T(1024)S(1)} %get-tuple-element.318, f32[13824]{0:T(1024)S(1)} %get-tuple-element.319), kind=kOutput, calls=%fused_computation.3.clone.1 | convolution fusion | flops 194641920 | bytes 8188416 | tf_op jit(solution)/shard_map/while/body/eval_jaxpr/dot_general | solution.py:42
  455.2 5.5 convolution_add_fusion.2
  469.8 3.7 fusion.77
  474.8 18.2 %convolution_multiply_fusion.3 = f32[13824,64]{0,1:T(8,128)} fusion(f32[18,13824]{1,0:T(8,128)} %mul.712, f32[64,18]{0,1:T(8,128)S(1)} %get-tuple-element.353, f32[13824,64]{0,1:T(8,128)S(1)} %fusion.77, f32[13824]{0:T(1024)S(1)} %get-tuple-element.318, f32[13824]{0:T(1024)S(1)} %get-tuple-element.319), kind=kOutput, calls=%fused_computation.3.clone.1 | convolution fusion | flops 194641920 | bytes 8188416 | tf_op jit(solution)/shard_map/while/body/eval_jaxpr/dot_general | solution.py:42
  493.0 5.5 convolution_add_fusion.2
  507.7 3.7 fusion.77
  512.7 18.2 %convolution_multiply_fusion.3 = f32[13824,64]{0,1:T(8,128)} fusion(f32[18,13824]{1,0:T(8,128)} %mul.712, f32[64,18]{0,1:T(8,128)S(1)} %get-tuple-element.353, f32[13824,64]{0,1:T(8,128)S(1)} %fusion.77, f32[13824]{0:T(1024)S(1)} %get-tuple-element.318, f32[13824]{0:T(1024)S(1)} %get-tuple-element.319), kind=kOutput, calls=%fused_computation.3.clone.1 | convolution fusion | flops 194641920 | bytes 8188416 | tf_op jit(solution)/shard_map/while/body/eval_jaxpr/dot_general | solution.py:42
  530.9 5.5 convolution_add_fusion.2
  545.6 3.7 fusion.77
  550.6 18.2 %convolution_multiply_fusion.3 = f32[13824,64]{0,1:T(8,128)} fusion(f32[18,13824]{1,0:T(8,128)} %mul.712, f32[64,18]{0,1:T(8,128)S(1)} %get-tuple-element.353, f32[13824,64]{0,1:T(8,128)S(1)} %fusion.77, f32[13824]{0:T(1024)S(1)} %get-tuple-element.318, f32[13824]{0:T(1024)S(1)} %get-tuple-element.319), kind=kOutput, calls=%fused_computation.3.clone.1 | convolution fusion | flops 194641920 | bytes 8188416 | tf_op jit(solution)/shard_map/while/body/eval_jaxpr/dot_general | solution.py:42
  568.8 5.5 convolution_add_fusion.2
  583.5 3.7 fusion.77
  588.5 18.2 %convolution_multiply_fusion.3 = f32[13824,64]{0,1:T(8,128)} fusion(f32[18,13824]{1,0:T(8,128)} %mul.712, f32[64,18]{0,1:T(8,128)S(1)} %get-tuple-element.353, f32[13824,64]{0,1:T(8,128)S(1)} %fusion.77, f32[13824]{0:T(1024)S(1)} %get-tuple-element.318, f32[13824]{0:T(1024)S(1)} %get-tuple-element.319), kind=kOutput, calls=%fused_computation.3.clone.1 | convolution fusion | flops 194641920 | bytes 8188416 | tf_op jit(solution)/shard_map/while/body/eval_jaxpr/dot_general | solution.py:42
  606.7 5.5 convolution_add_fusion.2
  621.4 3.7 fusion.77
  625.1 1.3 dynamic-slice_reduce_fusion.3
  626.4 18.2 %convolution_multiply_fusion.3 = f32[13824,64]{0,1:T(8,128)} fusion(f32[18,13824]{1,0:T(8,128)} %mul.712, f32[64,18]{0,1:T(8,128)S(1)} %get-tuple-element.353, f32[13824,64]{0,1:T(8,128)S(1)} %fusion.77, f32[13824]{0:T(1024)S(1)} %get-tuple-element.318, f32[13824]{0:T(1024)S(1)} %get-tuple-element.319), kind=kOutput, calls=%fused_computation.3.clone.1 | convolution fusion | flops 194641920 | bytes 8188416 | tf_op jit(solution)/shard_map/while/body/eval_jaxpr/dot_general | solution.py:42
  644.6 5.5 convolution_add_fusion.2
  650.2 4.9 psum.15
  (275 shorter events, 82.4 us)
Async XLA Ops:
  8.0 267.3 %copy-start = (s32[512]{0:T(512)S(1)}, s32[512]{0:T(512)}, u32[]{:S(2)}) copy-start(s32[512]{0:T(512)} %param.15) | copy-start | bytes 6148
  8.0 266.3 %sort.19.cloned.1.call-start = ((), (), s32[]{:S(2)}) async-start(), calls=%async_computation.1 | async-start | bytes 12320 | tf_op jit(solution)/shard_map/jit(argsort)/sort | solution.py:91
  9.9 329.0 %all-reduce.2.cloned.1.call-start = ((), (), s32[]{:S(2)}) async-start(), calls=%async_computation | async-start | bytes 3145728 | tf_op jit(solution)/shard_map/psum | solution.py:93
  101.1 9.1 %copy-start.8 = (s32[2,2]{1,0:T(2,128)S(1)}, s32[2,2]{1,0:T(2,128)}, u32[]{:S(2)}) copy-start(s32[2,2]{1,0:T(2,128)} %param.12) | copy-start | bytes 52
  255.1 11.6 %copy-start.9 = (f32[2]{0:T(128)S(1)}, f32[2]{0:T(128)}, u32[]{:S(2)}) copy-start(f32[2]{0:T(128)} %param.13) | copy-start | bytes 28
  270.5 3.6 copy-start.10
  270.5 3.6 copy-start.4
  270.6 3.6 copy-start.7
  347.0 6.4 copy-start.5
  356.1 3.7 copy-start.2
  356.1 3.7 copy-start.3
  379.4 5.5 copy-start.6
  379.4 5.5 copy-start.12
  384.9 6.4 copy-start.5
  394.0 3.7 copy-start.2
  394.0 3.7 copy-start.3
  417.3 5.5 copy-start.6
  417.3 5.5 copy-start.12
  422.8 6.4 copy-start.5
  431.9 3.7 copy-start.2
  431.9 3.7 copy-start.3
  455.2 5.5 copy-start.6
  455.2 5.5 copy-start.12
  460.7 6.4 copy-start.5
  469.8 3.7 copy-start.2
  469.8 3.7 copy-start.3
  493.0 5.5 copy-start.6
  493.0 5.5 copy-start.12
  498.6 6.4 copy-start.5
  507.7 3.7 copy-start.2
  507.7 3.7 copy-start.3
  530.9 5.5 copy-start.6
  530.9 5.5 copy-start.12
  536.5 6.4 copy-start.5
  545.6 3.7 copy-start.2
  545.6 3.7 copy-start.3
  568.8 5.5 copy-start.6
  568.8 5.5 copy-start.12
  574.4 6.4 copy-start.5
  583.5 3.7 copy-start.2
  583.5 3.7 copy-start.3
  606.7 5.5 copy-start.6
  606.7 5.5 copy-start.12
  612.3 6.4 copy-start.5
  621.3 3.7 copy-start.2
  621.4 3.7 copy-start.3
  644.6 5.5 copy-start.6
  644.6 5.5 copy-start.12
  (16 other events, 16.1 us)
Sparse Core Ops, SparseCore 0:
  11.7 2.2 sort.21.cloned.1.call-done
  (1 shorter events, 0.0 us)
Sparse Core Ops, SparseCore 1:
  274.1 64.8 all-reduce.1
where the time goes:
time: 668 us; the launch traced here: 663 us
  matrix products  255 us (38%)
  local copies, waits for them, and re-layouts  234 us (35%)
  other arithmetic  83.3 us (12%)
  waiting for transfers between devices  60.1 us (9%)
  between operations  15.7 us (2%)
  blocking collectives  9.31 us (1%)
    dot_general x8, matrix products, force_block(): smooth = jnp.dot(moments, form_table, precision=highest)  146 us
    psum x1, waiting for transfers between devices, shards(): summed = lax.psum(density_local, ('ka', 'ba'))  60.1 us
    unnamed x19, local copies, waits for them, and re-layouts  47.3 us
    reshape x1, local copies, waits for them, and re-layouts, shards(): coefficients.reshape(spin_count, complex_parts, kcount, bcount, atoms_blk...  45.4 us
    dot_general x8, matrix products, force_block(): return jnp.dot(smooth * wave_term, vectors, precision=highest)  44.3 us
    mul x1, local copies, waits for them, and re-layouts, shards(): masked = values * band_mask[:, None, :, :, None, None]  29.6 us
    dot_general x8, matrix products, force_block(): phases = jnp.dot(places, vectors.T, precision=highest)  29.6 us
    squeeze x2, local copies, waits for them, and re-layouts, shards(): masked[:, 1]  23.9 us
  transfers between devices with their start and end apart: 1, of which 1 were waited for; matrix products, arithmetic and copies ran while one was open for 1% of the time, Pallas kernels for 0%

commit v1 on v0

--- a/solution.py
+++ b/solution.py
@@ -90,7 +90,9 @@
     )
     ranking = jnp.argsort(owner_map.reshape(-1, atoms_blk), axis=1, stable=True)
     own_ranks = lax.dynamic_slice_in_dim(ranking, owner_index * per_owner, per_owner, 1)
-    summed = lax.psum(density_local, ("ka", "ba"))
+    summed = density_local
+    for dd in ("ka", "ba"):
+        summed = lax.psum(summed, dd)
     own_rows = lax.dynamic_index_in_dim(own_ranks, group_index, 0, keepdims=False)
     own_density = jnp.take(summed, own_rows, axis=2)
     block_count = own_ranks.shape[0]

time: 668 us -> 696 us (1.042)
  waiting for transfers between devices: 60.1 us -> 88.1 us
    psum x1 -> x2, waiting for transfers between devices: 60.1 us -> 88.1 us  [shards(): summed = lax.psum(summed, dd)]
  transfers between devices with their start and end apart: 1 -> 2, of which waited for: 1 -> 2; matrix products, arithmetic and copies ran while one was open for 1% -> 1% of each run, Pallas kernels for 0% -> 0%
where the time goes in v1:
time: 696 us; the launch traced here: 691 us
  matrix products  255 us (37%)
  local copies, waits for them, and re-layouts  234 us (34%)
  waiting for transfers between devices  88.1 us (13%)
  other arithmetic  83.3 us (12%)
  between operations  15.8 us (2%)
  blocking collectives  9.31 us (1%)
    dot_general x8, matrix products, force_block(): smooth = jnp.dot(moments, form_table, precision=highest)  146 us
    psum x2, waiting for transfers between devices, shards(): summed = lax.psum(summed, dd)  88.1 us
    unnamed x19, local copies, waits for them, and re-layouts  47.3 us
    reshape x1, local copies, waits for them, and re-layouts, shards(): coefficients.reshape(spin_count, complex_parts, kcount, bcount, atoms_blk...  45.4 us
    dot_general x8, matrix products, force_block(): return jnp.dot(smooth * wave_term, vectors, precision=highest)  44.3 us
    mul x1, local copies, waits for them, and re-layouts, shards(): masked = values * band_mask[:, None, :, :, None, None]  29.6 us
    dot_general x8, matrix products, force_block(): phases = jnp.dot(places, vectors.T, precision=highest)  29.6 us
    squeeze x2, local copies, waits for them, and re-layouts, shards(): masked[:, 1]  23.9 us
  transfers between devices with their start and end apart: 2, of which 2 were waited for; matrix products, arithmetic and copies ran while one was open for 1% of the time, Pallas kernels for 0%

profile of v1, /device:TPU:0, one launch (start us, length us, event | category | flops | bytes accessed | tf_op | source)
XLA Modules:
  0.0 691.2 jit_solution(6792068242337037878)
XLA Ops:
  10.0 45.7 %copy.45 = bf16[2,2,2,256,4608]{3,2,4,1,0:T(2,128)(2,1)} copy(bf16[2,2,2,256,4608]{4,3,2,1,0:T(8,128)(2,1)} %param.11) | data formatting | bytes 37748736 | tf_op args[0]
  55.7 45.4 %copy.46 = bf16[2,2,2,256,256,18]{4,3,5,2,1,0:T(8,128)(2,1)} copy(bf16[2,2,2,256,256,18]{3,2,5,4,1,0:T(2,128)(2,1)} %bitcast.68) | data formatting | bytes 37748736 | tf_op jit(solution)/shard_map/reshape | solution.py:78
  101.1 9.1 %slice.35 = bf16[2,1,2,256,256,18]{3,2,5,4,1,0:T(2,128)(2,1)} slice(bf16[2,2,2,256,256,18]{3,2,5,4,1,0:T(2,128)(2,1)} %bitcast.69), slice={[0:2], [0:1], [0:2], [0:256], [0:256], [0:18]} | slice | bytes 18874368 | tf_op jit(solution)/shard_map/slice | solution.py:84
  110.3 16.7 %broadcast_multiply_fusion.2 = bf16[2,2,2,256,256,18]{4,3,5,2,1,0:T(8,128)(2,1)} fusion(bf16[2,2,2,256,256,18]{4,3,5,2,1,0:T(8,128)(2,1)} %copy.46, bf16[2,2,256]{2,1,0:T(2,128)(2,1)S(1)} %compare_convert_fusion), kind=kLoop, calls=%fused_computation.84 | loop fusion | flops 9437184 | bytes 37750784 | tf_op jit(solution)/shard_map/mul | solution.py:79
  127.0 8.4 %slice_bitcast_fusion = bf16[2,2,256,256,18]{3,2,4,1,0:T(8,128)(2,1)} fusion(bf16[2,2,2,256,256,18]{4,3,5,2,1,0:T(8,128)(2,1)} %broadcast_multiply_fusion.2), kind=kLoop, calls=%fused_computation.83 | loop fusion | bytes 18874368 | tf_op jit(solution)/shard_map/squeeze | solution.py:84
  135.4 29.6 %copy.62 = bf16[2,2,2,256,256,18]{3,5,1,2,0,4:T(8,128)(2,1)} copy(bf16[2,2,2,256,256,18]{4,3,5,2,1,0:T(8,128)(2,1)} %broadcast_multiply_fusion.2) | data formatting | bytes 37748736 | tf_op jit(solution)/shard_map/mul | solution.py:79
  165.1 15.5 %copy.50 = bf16[2,2,256,256,18]{2,4,3,1,0:T(8,128)(2,1)} copy(bf16[2,2,256,256,18]{3,2,4,1,0:T(8,128)(2,1)} %slice_bitcast_fusion) | data formatting | bytes 18874368 | tf_op jit(solution)/shard_map/squeeze | solution.py:84
  180.6 13.3 %fusion.40 = f32[2,2,256,18,18]{4,3,2,1,0:T(8,128)} fusion(bf16[2,2,256,256,18]{2,4,3,1,0:T(8,128)(2,1)} %copy.50, bf16[2,1,2,256,256,18]{3,2,5,4,1,0:T(2,128)(2,1)} %slice.35), kind=kOutput, calls=%fused_computation.80 | convolution fusion | flops 169869312 | bytes 20201472 | tf_op jit(solution)/shard_map/skbai,skbaj->skaij/dot_general | solution.py:83
  193.9 14.0 %copy.51 = f32[2,2,256,18,18]{3,4,2,1,0:T(8,128)} copy(f32[2,2,256,18,18]{4,3,2,1,0:T(8,128)} %fusion.40) | data formatting | bytes 2654208 | tf_op jit(solution)/shard_map/skbai,skbaj->skaij/dot_general | solution.py:83
  207.9 14.1 %fusion.41 = f32[2,1,2,256,18,18]{5,4,3,2,0,1:T(8,128)} fusion(f32[2,2,256,18,18]{4,3,2,1,0:T(8,128)} %fusion.40, f32[2,2,256,18,18]{3,4,2,1,0:T(8,128)} %copy.51), kind=kLoop, calls=%fused_computation.82 | loop fusion | flops 331776 | bytes 3981312 | tf_op jit(solution)/shard_map/stack | solution.py:87
  221.9 11.4 %copy.53 = f32[2,1,2,256,18,18]{3,2,5,4,1,0:T(2,128)S(1)} copy(f32[2,1,2,256,18,18]{5,4,3,2,0,1:T(8,128)} %fusion.41) | data formatting | bytes 2654208 | tf_op jit(solution)/shard_map/stack | solution.py:87
  233.4 21.8 %fusion.42 = f32[2,1,2,256,18,18]{4,5,2,0,3,1:T(8,128)} fusion(bf16[2,2,2,256,256,18]{3,5,1,2,0,4:T(8,128)(2,1)} %copy.62, bf16[2,2,2,256,256,18]{3,2,5,4,1,0:T(2,128)(2,1)} %bitcast.70), kind=kOutput, calls=%fused_computation.85 | convolution fusion | flops 339738624 | bytes 39075840 | tf_op jit(solution)/shard_map/sckbai,sckbaj->skaij/dot_general | solution.py:80
  255.1 11.6 %copy.52 = f32[2,1,2,256,18,18]{3,2,5,4,1,0:T(2,128)S(1)} copy(f32[2,1,2,256,18,18]{4,5,2,0,3,1:T(8,128)} %fusion.42) | data formatting | bytes 2654208 | tf_op jit(solution)/shard_map/stack | solution.py:87
  266.8 3.7 fusion.45
  271.6 2.4 copy.56
  276.1 69.6 %all-reduce.3.cloned.1.call-done = f32[2,2,256,324]{3,1,2,0:T(2,128)} async-done(((f32[2,2,256,324]{3,1,2,0:T(2,128)}), f32[2,2,256,324]{3,1,2,0:T(2,128)}) %all-reduce.3.cloned.1.call-update) | async-done | bytes 1327120 | tf_op jit(solution)/shard_map/psum | solution.py:95
  348.6 18.5 %all-reduce.5.cloned.1.call-done = f32[2,2,256,324]{3,1,2,0:T(2,128)} async-done(((f32[2,2,256,324]{3,1,2,0:T(2,128)}), f32[2,2,256,324]{3,1,2,0:T(2,128)}) %all-reduce.5.cloned.1.call-update) | async-done | bytes 1327120 | tf_op jit(solution)/shard_map/psum | solution.py:95
  367.1 2.2 gather_fusion
  370.5 4.4 all-gather
  374.9 303.2 %while.14 = (s32[]{:T(128)}, f32[64,3]{0,1:T(4,128)}, f32[2,1]{0,1:T(1,128)S(1)}, s32[8]{0:T(128)S(1)}, s32[]{:T(128)}, /*index=5*/f32[64,18]{0,1:T(8,128)S(1)},...) while((s32[]{:T(128)}, f32[64,3]{0,1:T(4,128)}, ...), condition=%wide.region_6.7_spmd.clone, body=%wide.region_5.6_spmd.clone.sunk | while | flops 262103424 | bytes 21960220 | solution.py:59
  384.2 3.7 fusion.77
  387.9 1.3 dynamic-slice_reduce_fusion.3
  389.3 18.2 %convolution_multiply_fusion.3 = f32[13824,64]{0,1:T(8,128)} fusion(f32[18,13824]{1,0:T(8,128)} %mul.712, f32[64,18]{0,1:T(8,128)S(1)} %get-tuple-element.353, f32[13824,64]{0,1:T(8,128)S(1)} %fusion.77, f32[13824]{0:T(1024)S(1)} %get-tuple-element.318, f32[13824]{0:T(1024)S(1)} %get-tuple-element.319), kind=kOutput, calls=%fused_computation.3.clone.1 | convolution fusion | flops 194641920 | bytes 8188416 | tf_op jit(solution)/shard_map/while/body/eval_jaxpr/dot_general | solution.py:42
  407.5 5.5 convolution_add_fusion.2
  422.1 3.7 fusion.77
  425.8 1.3 dynamic-slice_reduce_fusion.3
  427.1 18.2 %convolution_multiply_fusion.3 = f32[13824,64]{0,1:T(8,128)} fusion(f32[18,13824]{1,0:T(8,128)} %mul.712, f32[64,18]{0,1:T(8,128)S(1)} %get-tuple-element.353, f32[13824,64]{0,1:T(8,128)S(1)} %fusion.77, f32[13824]{0:T(1024)S(1)} %get-tuple-element.318, f32[13824]{0:T(1024)S(1)} %get-tuple-element.319), kind=kOutput, calls=%fused_computation.3.clone.1 | convolution fusion | flops 194641920 | bytes 8188416 | tf_op jit(solution)/shard_map/while/body/eval_jaxpr/dot_general | solution.py:42
  445.3 5.5 convolution_add_fusion.2
  460.0 3.7 fusion.77
  463.7 1.3 dynamic-slice_reduce_fusion.3
  465.0 18.2 %convolution_multiply_fusion.3 = f32[13824,64]{0,1:T(8,128)} fusion(f32[18,13824]{1,0:T(8,128)} %mul.712, f32[64,18]{0,1:T(8,128)S(1)} %get-tuple-element.353, f32[13824,64]{0,1:T(8,128)S(1)} %fusion.77, f32[13824]{0:T(1024)S(1)} %get-tuple-element.318, f32[13824]{0:T(1024)S(1)} %get-tuple-element.319), kind=kOutput, calls=%fused_computation.3.clone.1 | convolution fusion | flops 194641920 | bytes 8188416 | tf_op jit(solution)/shard_map/while/body/eval_jaxpr/dot_general | solution.py:42
  483.2 5.5 convolution_add_fusion.2
  497.9 3.7 fusion.77
  502.9 18.2 %convolution_multiply_fusion.3 = f32[13824,64]{0,1:T(8,128)} fusion(f32[18,13824]{1,0:T(8,128)} %mul.712, f32[64,18]{0,1:T(8,128)S(1)} %get-tuple-element.353, f32[13824,64]{0,1:T(8,128)S(1)} %fusion.77, f32[13824]{0:T(1024)S(1)} %get-tuple-element.318, f32[13824]{0:T(1024)S(1)} %get-tuple-element.319), kind=kOutput, calls=%fused_computation.3.clone.1 | convolution fusion | flops 194641920 | bytes 8188416 | tf_op jit(solution)/shard_map/while/body/eval_jaxpr/dot_general | solution.py:42
  521.1 5.5 convolution_add_fusion.2
  535.7 3.7 fusion.77
  540.8 18.2 %convolution_multiply_fusion.3 = f32[13824,64]{0,1:T(8,128)} fusion(f32[18,13824]{1,0:T(8,128)} %mul.712, f32[64,18]{0,1:T(8,128)S(1)} %get-tuple-element.353, f32[13824,64]{0,1:T(8,128)S(1)} %fusion.77, f32[13824]{0:T(1024)S(1)} %get-tuple-element.318, f32[13824]{0:T(1024)S(1)} %get-tuple-element.319), kind=kOutput, calls=%fused_computation.3.clone.1 | convolution fusion | flops 194641920 | bytes 8188416 | tf_op jit(solution)/shard_map/while/body/eval_jaxpr/dot_general | solution.py:42
  559.0 5.5 convolution_add_fusion.2
  573.6 3.7 fusion.77
  578.7 18.2 %convolution_multiply_fusion.3 = f32[13824,64]{0,1:T(8,128)} fusion(f32[18,13824]{1,0:T(8,128)} %mul.712, f32[64,18]{0,1:T(8,128)S(1)} %get-tuple-element.353, f32[13824,64]{0,1:T(8,128)S(1)} %fusion.77, f32[13824]{0:T(1024)S(1)} %get-tuple-element.318, f32[13824]{0:T(1024)S(1)} %get-tuple-element.319), kind=kOutput, calls=%fused_computation.3.clone.1 | convolution fusion | flops 194641920 | bytes 8188416 | tf_op jit(solution)/shard_map/while/body/eval_jaxpr/dot_general | solution.py:42
  596.9 5.5 convolution_add_fusion.2
  611.5 3.7 fusion.77
  616.5 18.2 %convolution_multiply_fusion.3 = f32[13824,64]{0,1:T(8,128)} fusion(f32[18,13824]{1,0:T(8,128)} %mul.712, f32[64,18]{0,1:T(8,128)S(1)} %get-tuple-element.353, f32[13824,64]{0,1:T(8,128)S(1)} %fusion.77, f32[13824]{0:T(1024)S(1)} %get-tuple-element.318, f32[13824]{0:T(1024)S(1)} %get-tuple-element.319), kind=kOutput, calls=%fused_computation.3.clone.1 | convolution fusion | flops 194641920 | bytes 8188416 | tf_op jit(solution)/shard_map/while/body/eval_jaxpr/dot_general | solution.py:42
  634.7 5.5 convolution_add_fusion.2
  649.4 3.7 fusion.77
  654.4 18.2 %convolution_multiply_fusion.3 = f32[13824,64]{0,1:T(8,128)} fusion(f32[18,13824]{1,0:T(8,128)} %mul.712, f32[64,18]{0,1:T(8,128)S(1)} %get-tuple-element.353, f32[13824,64]{0,1:T(8,128)S(1)} %fusion.77, f32[13824]{0:T(1024)S(1)} %get-tuple-element.318, f32[13824]{0:T(1024)S(1)} %get-tuple-element.319), kind=kOutput, calls=%fused_computation.3.clone.1 | convolution fusion | flops 194641920 | bytes 8188416 | tf_op jit(solution)/shard_map/while/body/eval_jaxpr/dot_general | solution.py:42
  672.6 5.5 convolution_add_fusion.2
  678.2 4.9 psum.23
  (278 shorter events, 83.8 us)
Async XLA Ops:
  8.0 267.3 %copy-start = (s32[512]{0:T(512)S(1)}, s32[512]{0:T(512)}, u32[]{:S(2)}) copy-start(s32[512]{0:T(512)} %param.15) | copy-start | bytes 6148
  8.0 266.4 %sort.19.cloned.1.call-start = ((), (), s32[]{:S(2)}) async-start(), calls=%async_computation.2 | async-start | bytes 12320 | tf_op jit(solution)/shard_map/jit(argsort)/sort | solution.py:91
  9.9 335.7 %all-reduce.3.cloned.1.call-start = ((), (), s32[]{:S(2)}) async-start(), calls=%async_computation | async-start | bytes 3145728 | tf_op jit(solution)/shard_map/psum | solution.py:95
  101.1 9.1 %copy-start.8 = (s32[2,2]{1,0:T(2,128)S(1)}, s32[2,2]{1,0:T(2,128)}, u32[]{:S(2)}) copy-start(s32[2,2]{1,0:T(2,128)} %param.12) | copy-start | bytes 52
  255.1 11.6 %copy-start.9 = (f32[2]{0:T(128)S(1)}, f32[2]{0:T(128)}, u32[]{:S(2)}) copy-start(f32[2]{0:T(128)} %param.13) | copy-start | bytes 28
  270.6 3.8 copy-start.10
  274.1 93.0 %all-reduce.5.cloned.1.call-start = ((), (), s32[]{:S(2)}) async-start(), calls=%async_computation.1 | async-start | bytes 3145728 | tf_op jit(solution)/shard_map/psum | solution.py:95
  375.1 7.8 %copy-start.5 = (f32[2,1]{0,1:T(1,128)}, f32[2,1]{0,1:T(1,128)S(1)}, u32[]{:S(2)}) copy-start(f32[2,1]{0,1:T(1,128)S(1)} %get-tuple-element.350) | copy-start | bytes 28 | tf_op jit(solution)/shard_map/while
  375.1 7.8 %copy-start.11 = (s32[8]{0:T(128)}, s32[8]{0:T(128)S(1)}, u32[]{:S(2)}) copy-start(s32[8]{0:T(128)S(1)} %get-tuple-element.351) | copy-start | bytes 100 | tf_op jit(solution)/shard_map/while
  384.2 3.7 copy-start.2
  384.2 3.7 copy-start.3
  407.5 5.5 copy-start.6
  407.5 5.5 copy-start.12
  413.0 7.8 %copy-start.5 = (f32[2,1]{0,1:T(1,128)}, f32[2,1]{0,1:T(1,128)S(1)}, u32[]{:S(2)}) copy-start(f32[2,1]{0,1:T(1,128)S(1)} %get-tuple-element.350) | copy-start | bytes 28 | tf_op jit(solution)/shard_map/while
  413.0 7.8 %copy-start.11 = (s32[8]{0:T(128)}, s32[8]{0:T(128)S(1)}, u32[]{:S(2)}) copy-start(s32[8]{0:T(128)S(1)} %get-tuple-element.351) | copy-start | bytes 100 | tf_op jit(solution)/shard_map/while
  422.1 3.7 copy-start.2
  422.1 3.7 copy-start.3
  445.3 5.5 copy-start.6
  445.3 5.5 copy-start.12
  450.9 7.8 %copy-start.5 = (f32[2,1]{0,1:T(1,128)}, f32[2,1]{0,1:T(1,128)S(1)}, u32[]{:S(2)}) copy-start(f32[2,1]{0,1:T(1,128)S(1)} %get-tuple-element.350) | copy-start | bytes 28 | tf_op jit(solution)/shard_map/while
  450.9 7.8 %copy-start.11 = (s32[8]{0:T(128)}, s32[8]{0:T(128)S(1)}, u32[]{:S(2)}) copy-start(s32[8]{0:T(128)S(1)} %get-tuple-element.351) | copy-start | bytes 100 | tf_op jit(solution)/shard_map/while
  459.9 3.7 copy-start.2
  460.0 3.7 copy-start.3
  483.2 5.5 copy-start.6
  483.2 5.5 copy-start.12
  488.8 7.8 %copy-start.5 = (f32[2,1]{0,1:T(1,128)}, f32[2,1]{0,1:T(1,128)S(1)}, u32[]{:S(2)}) copy-start(f32[2,1]{0,1:T(1,128)S(1)} %get-tuple-element.350) | copy-start | bytes 28 | tf_op jit(solution)/shard_map/while
  488.8 7.8 %copy-start.11 = (s32[8]{0:T(128)}, s32[8]{0:T(128)S(1)}, u32[]{:S(2)}) copy-start(s32[8]{0:T(128)S(1)} %get-tuple-element.351) | copy-start | bytes 100 | tf_op jit(solution)/shard_map/while
  521.1 5.5 copy-start.6
  521.1 5.5 copy-start.12
  526.6 7.8 %copy-start.5 = (f32[2,1]{0,1:T(1,128)}, f32[2,1]{0,1:T(1,128)S(1)}, u32[]{:S(2)}) copy-start(f32[2,1]{0,1:T(1,128)S(1)} %get-tuple-element.350) | copy-start | bytes 28 | tf_op jit(solution)/shard_map/while
  526.6 7.8 %copy-start.11 = (s32[8]{0:T(128)}, s32[8]{0:T(128)S(1)}, u32[]{:S(2)}) copy-start(s32[8]{0:T(128)S(1)} %get-tuple-element.351) | copy-start | bytes 100 | tf_op jit(solution)/shard_map/while
  535.7 3.7 copy-start.2
  535.7 3.7 copy-start.3
  559.0 5.5 copy-start.6
  559.0 5.5 copy-start.12
  564.5 7.8 %copy-start.5 = (f32[2,1]{0,1:T(1,128)}, f32[2,1]{0,1:T(1,128)S(1)}, u32[]{:S(2)}) copy-start(f32[2,1]{0,1:T(1,128)S(1)} %get-tuple-element.350) | copy-start | bytes 28 | tf_op jit(solution)/shard_map/while
  564.5 7.8 %copy-start.11 = (s32[8]{0:T(128)}, s32[8]{0:T(128)S(1)}, u32[]{:S(2)}) copy-start(s32[8]{0:T(128)S(1)} %get-tuple-element.351) | copy-start | bytes 100 | tf_op jit(solution)/shard_map/while
  573.6 3.7 copy-start.2
  596.9 5.5 copy-start.6
  596.9 5.5 copy-start.12
  602.4 7.8 %copy-start.5 = (f32[2,1]{0,1:T(1,128)}, f32[2,1]{0,1:T(1,128)S(1)}, u32[]{:S(2)}) copy-start(f32[2,1]{0,1:T(1,128)S(1)} %get-tuple-element.350) | copy-start | bytes 28 | tf_op jit(solution)/shard_map/while
  602.4 7.8 %copy-start.11 = (s32[8]{0:T(128)}, s32[8]{0:T(128)S(1)}, u32[]{:S(2)}) copy-start(s32[8]{0:T(128)S(1)} %get-tuple-element.351) | copy-start | bytes 100 | tf_op jit(solution)/shard_map/while
  634.7 5.5 copy-start.6
  634.7 5.5 copy-start.12
  640.3 7.8 %copy-start.5 = (f32[2,1]{0,1:T(1,128)}, f32[2,1]{0,1:T(1,128)S(1)}, u32[]{:S(2)}) copy-start(f32[2,1]{0,1:T(1,128)S(1)} %get-tuple-element.350) | copy-start | bytes 28 | tf_op jit(solution)/shard_map/while
  640.3 7.8 %copy-start.11 = (s32[8]{0:T(128)}, s32[8]{0:T(128)S(1)}, u32[]{:S(2)}) copy-start(s32[8]{0:T(128)S(1)} %get-tuple-element.351) | copy-start | bytes 100 | tf_op jit(solution)/shard_map/while
  672.6 5.5 copy-start.6
  672.6 5.5 copy-start.12
  (17 other events, 40.2 us)
Sparse Core Ops, SparseCore 0:
  11.7 2.2 sort.21.cloned.1.call-done
  (1 shorter events, 0.0 us)
Sparse Core Ops, SparseCore 1:
  274.1 71.4 all-reduce.2
  347.8 19.2 all-reduce.4
